TPU v7x, 128 devices: a whole 4x4x4 slice. The times are simulated.
128 devices in a mesh: seq: 32 (over y, z, core), head: 4 (over x).
Axes of the slice: x: 4, y: 4, z: 4, core: 2. Of those that a mesh axis runs over, the one named last changes fastest.
Arguments:
- vision: bfloat16 [65536, 7680], P(('seq', 'head')), may hold values from -6 to 6
- w_key: bfloat16 [7680, 512], replicated, may hold values from -0.0625 to 0.0625
- w_value: bfloat16 [7680, 512], replicated, may hold values from -0.0625 to 0.0625
- queries: bfloat16 [256, 4096], P('seq', 'head'), may hold values from -240 to 240
- w_out: bfloat16 [4096, 8192], P('head', 'seq'), may hold values from -0.09375 to 0.09375
Outputs:
- mixed: bfloat16 [256, 8192], P('head', 'seq')
All inputs are finite; a program needn't handle non-finite values.
Results may differ from a plain program's by a relative error of at most 0.03.
Values may be sent and summed in bfloat16 or wider, within the bound.
No kernel may reach another device: no remote copies, remote signals or barrier semaphores. Data moves between devices by JAX's collectives and lax.ppermute only.
A program may use at most 128 MiB of HBM per device.

v0:
```python
import jax
import jax.numpy as jnp
from jax import lax
from jax.sharding import PartitionSpec as P

HD = 128


def scale_rows(partial_value, factor):
    return (
        partial_value.reshape(factor.shape[0], factor.shape[1], -1) * factor[:, :, None]
    ).reshape(factor.shape[0], -1)


def divide_rows(partial_value, denom):
    return (partial_value.reshape(denom.shape[0], denom.shape[1], -1) / denom[:, :, None]).reshape(
        denom.shape[0], -1
    )


def attend(queries_all, keys_here, values_here):
    head_size = HD
    kv_local = keys_here.shape[1] // head_size
    text_rows = queries_all.shape[0]
    q_heads = queries_all.shape[1] // head_size
    group_size = q_heads // kv_local
    grouped = queries_all.reshape(text_rows, kv_local, group_size, head_size)
    key_heads = keys_here.reshape(keys_here.shape[0], kv_local, head_size)
    value_heads = values_here.reshape(values_here.shape[0], kv_local, head_size)
    scores = jnp.einsum(
        "tkgd,nkd->kgtn", grouped, key_heads, preferred_element_type=jnp.float32
    ) * head_size ** (-0.5)
    maxima = jnp.max(scores, axis=-1)
    powers = jnp.exp(scores - maxima[..., None])
    totals = jnp.sum(powers, axis=-1)
    partial_value = jnp.einsum(
        "kgtn,nkd->tkgd",
        powers.astype(jnp.bfloat16),
        value_heads,
        preferred_element_type=jnp.float32,
    )
    partial_value = partial_value.reshape(text_rows, q_heads * head_size)
    maxima = maxima.transpose(2, 0, 1).reshape(text_rows, q_heads)
    totals = totals.transpose(2, 0, 1).reshape(text_rows, q_heads)
    return (maxima, totals, partial_value)


def shards(vision, w_key, w_value, queries, w_out):
    keys = jnp.dot(vision, w_key, preferred_element_type=jnp.float32).astype(jnp.bfloat16)
    values = jnp.dot(vision, w_value, preferred_element_type=jnp.float32).astype(jnp.bfloat16)
    keys_here, values_here = (
        lax.all_to_all(keys, "head", split_axis=1, concat_axis=0, tiled=True),
        lax.all_to_all(values, "head", split_axis=1, concat_axis=0, tiled=True),
    )
    queries_all = lax.all_gather(queries, "seq", axis=0, tiled=True)
    maxima, totals, partial_value = attend(queries_all, keys_here, values_here)
    global_max = lax.pmax(maxima, "seq")
    factor = jnp.exp(maxima - global_max)
    denom, numer = (
        lax.psum((totals * factor).astype(jnp.bfloat16), "seq").astype(jnp.float32),
        lax.psum(scale_rows(partial_value, factor).astype(jnp.bfloat16), "seq").astype(jnp.float32),
    )
    attended = divide_rows(numer, denom).astype(jnp.bfloat16)
    return lax.psum_scatter(
        jnp.dot(attended, w_out, preferred_element_type=jnp.float32).astype(jnp.bfloat16),
        "head",
        scatter_dimension=0,
        tiled=True,
    )


def solution(mesh):
    placed = (P(("seq", "head"), None), P(), P(), P("seq", "head"), P("head", "seq"))
    return jax.shard_map(
        shards, mesh=mesh, in_specs=placed, out_specs=P("head", "seq"), check_vma=False
    )
```

profile of v0, /device:TPU:0, one launch (start us, length us, event | category | flops | bytes accessed | tf_op | source)
XLA Modules:
  0.0 286.8 jit_solution(6718358822578115209)
XLA Ops:
  6.5 0.0 copy-start
  6.5 10.6 %convolution_convert_fusion.1 = bf16[512,512]{0,1:T(8,128)(2,1)} fusion(bf16[512,7680]{1,0:T(8,128)(2,1)} %param.5, bf16[7680,512]{1,0:T(8,128)(2,1)} %param.7), kind=kOutput, calls=%fused_computation.8 | convolution fusion | flops 4026793984 | bytes 16252928 | tf_op jit(solution)/shard_map/dot_general | solution.py:50
  17.1 0.0 copy-start.1
  17.1 4.5 %all-to-all-start = ((bf16[512,4,128]{0,2,1:T(8,128)(2,1)}), bf16[512,4,128]{0,2,1:T(8,128)(2,1)S(1)}, u32[]{:S(2)}, u32[]{:S(2)}) async-start(bf16[512,4,128]{0,2,1:T(8,128)(2,1)} %bitcast), calls=%async_computation | async-start | bytes 1048576 | tf_op jit(solution)/shard_map/all_to_all | solution.py:53
  21.7 10.5 %convolution_convert_fusion = bf16[512,512]{0,1:T(8,128)(2,1)} fusion(bf16[512,7680]{1,0:T(8,128)(2,1)} %param.5, bf16[7680,512]{1,0:T(8,128)(2,1)} %param.6), kind=kOutput, calls=%fused_computation.7 | convolution fusion | flops 4026793984 | bytes 16252928 | tf_op jit(solution)/shard_map/dot_general | solution.py:49
  32.2 0.0 all-to-all-done
  32.2 4.8 %all-to-all-start.1 = ((bf16[512,4,128]{0,2,1:T(8,128)(2,1)}), bf16[512,4,128]{0,2,1:T(8,128)(2,1)S(1)}, u32[]{:S(2)}, u32[]{:S(2)}) async-start(bf16[512,4,128]{0,2,1:T(8,128)(2,1)} %bitcast.2), calls=%async_computation.1 | async-start | bytes 1048576 | tf_op jit(solution)/shard_map/all_to_all | solution.py:52
  37.0 0.0 all-reduce.2.cloned.1.call-start
  37.0 0.0 copy-done.1
  37.0 26.5 %all_gather.3 = bf16[256,1024]{1,0:T(8,128)(2,1)S(1)} all-gather(bf16[8,1024]{1,0:T(8,128)(2,1)S(1)} %copy-done.1), channel_id=1, replica_groups=mesh['seq'=32,'head'=4] {'seq'}, dimensions={0}, use_global_device_ids=true | all-gather | bytes 540672 | tf_op jit(solution)/shard_map/all_gather | solution.py:55
  63.5 0.2 copy.16
  63.7 0.4 copy.14
  64.1 0.4 reshape.57
  64.5 0.0 all-to-all-done.1
  64.5 0.3 copy.15
  64.8 8.0 %bitcast_reduce_fusion = (f32[8,256]{1,0:T(8,128)S(1)}, f32[2048,256,8]{1,0,2:T(8,128)}) fusion(bf16[2048,128,1]{1,0,2:T(8,128)(2,1)S(1)} %bitcast.66, bf16[256,8,128]{0,2,1:T(8,128)(2,1)S(1)} %bitcast.65), kind=kOutput, calls=%fused_computation.1 | convolution fusion | flops 1082128384 | bytes 17833984 | tf_op jit(solution)/shard_map/tkgd,nkd->kgtn/dot_general | solution.py:30
  72.8 8.5 %fusion.1 = f32[8,256]{1,0:T(8,128)S(1)} fusion(f32[2048,256,8]{1,0,2:T(8,128)} %get-tuple-element.8, f32[8,256]{1,0:T(8,128)S(1)} %get-tuple-element.7), kind=kLoop, calls=%fused_computation.3 | loop fusion | flops 12580864 | bytes 16793600 | tf_op jit(solution)/shard_map/reduce_sum | solution.py:35
  81.3 7.4 %fusion.4 = f32[128,8,256]{2,0,1:T(8,128)S(1)} fusion(bf16[2048,128,1]{0,1,2:T(8,128)(2,1)S(1)} %reshape.57, f32[2048,256,8]{1,0,2:T(8,128)} %get-tuple-element.8, f32[8,256]{1,0:T(8,128)S(1)} %get-tuple-element.7), kind=kOutput, calls=%fused_computation.6 | convolution fusion | flops 1086324736 | bytes 18358272 | tf_op jit(solution)/shard_map/kgtn,nkd->tkgd/dot_general | solution.py:36
  88.7 66.3 %pmax.7 = f32[256,8]{0,1:T(8,128)S(1)} all-reduce(f32[256,8]{0,1:T(8,128)S(1)} %bitcast.69), channel_id=1, replica_groups=mesh['seq'=32,'head'=4] {'seq'}, use_global_device_ids=true, to_apply=%region_1.0 | all-reduce | flops 2048 | bytes 16384 | tf_op jit(solution)/shard_map/pmax | solution.py:57
  155.1 0.9 fusion.6
  156.0 0.0 all-reduce.2.cloned.1.call-update
  156.0 0.0 reduce-scatter.2.cloned.1.call-start
  156.0 62.8 %psum.15 = bf16[256,8]{0,1:T(8,128)(2,1)S(1)} all-reduce(bf16[256,8]{0,1:T(8,128)(2,1)S(1)} %get-tuple-element.5), channel_id=1, replica_groups=mesh['seq'=32,'head'=4] {'seq'}, use_global_device_ids=true, to_apply=%region_4.0 | all-reduce | flops 2048 | bytes 8192 | tf_op jit(solution)/shard_map/psum | solution.py:60
  218.8 38.6 %all-reduce.2.cloned.1.call-done = bf16[256,1024]{0,1:T(8,128)(2,1)} async-done(((bf16[256,1024]{0,1:T(8,128)(2,1)}), bf16[256,1024]{0,1:T(8,128)(2,1)}) %all-reduce.2.cloned.1.call-update) | async-done | bytes 524304 | tf_op jit(solution)/shard_map/psum | solution.py:61
  257.4 1.1 fusion.7
  258.6 0.0 copy-done
  258.6 1.0 convolution_convert_fusion.2
  259.6 0.0 reduce-scatter.2.cloned.1.call-update
  259.6 20.4 %reduce-scatter.2.cloned.1.call-done = bf16[64,256]{1,0:T(8,128)(2,1)} async-done(((bf16[256,256]{1,0:T(8,128)(2,1)}), bf16[64,256]{1,0:T(8,128)(2,1)}) %reduce-scatter.2.cloned.1.call-update) | async-done | bytes 32784 | tf_op jit(solution)/shard_map/reduce_scatter | solution.py:64
  (2 shorter events, 0.0 us)
Async XLA Ops:
  6.5 252.0 %copy-start = (bf16[1024,256]{1,0:T(8,128)(2,1)S(1)}, bf16[1024,256]{1,0:T(8,128)(2,1)}, u32[]{:S(2)}) copy-start(bf16[1024,256]{1,0:T(8,128)(2,1)} %param.9) | copy-start | bytes 1572868
  17.1 19.9 %copy-start.1 = (bf16[8,1024]{1,0:T(8,128)(2,1)S(1)}, bf16[8,1024]{1,0:T(8,128)(2,1)}, u32[]{:S(2)}) copy-start(bf16[8,1024]{1,0:T(8,128)(2,1)} %param.8) | copy-start | bytes 49156
  17.1 15.1 %all-to-all-start = ((bf16[512,4,128]{0,2,1:T(8,128)(2,1)}), bf16[512,4,128]{0,2,1:T(8,128)(2,1)S(1)}, u32[]{:S(2)}, u32[]{:S(2)}) async-start(bf16[512,4,128]{0,2,1:T(8,128)(2,1)} %bitcast), calls=%async_computation | async-start | bytes 1048576 | tf_op jit(solution)/shard_map/all_to_all | solution.py:53
  32.2 32.3 %all-to-all-start.1 = ((bf16[512,4,128]{0,2,1:T(8,128)(2,1)}), bf16[512,4,128]{0,2,1:T(8,128)(2,1)S(1)}, u32[]{:S(2)}, u32[]{:S(2)}) async-start(bf16[512,4,128]{0,2,1:T(8,128)(2,1)} %bitcast.2), calls=%async_computation.1 | async-start | bytes 1048576 | tf_op jit(solution)/shard_map/all_to_all | solution.py:52
  37.0 220.4 %all-reduce.2.cloned.1.call-start = ((), (), s32[]{:S(2)}) async-start(), calls=%async_computation.3 | async-start | bytes 1048576 | tf_op jit(solution)/shard_map/psum | solution.py:61
  156.0 124.0 %reduce-scatter.2.cloned.1.call-start = ((), (), s32[]{:S(2)}) async-start(), calls=%async_computation.4 | async-start | bytes 163840 | tf_op jit(solution)/shard_map/reduce_scatter | solution.py:64
Sparse Core Ops, SparseCore 0:
  156.1 101.2 all-reduce.1
  259.8 20.1 reduce-scatter.1
where the time goes:
time: 287 us
  blocking collectives  156 us (54%)
  waiting for transfers between devices  59 us (21%)
  matrix products  37.6 us (13%)
  between operations  13.5 us (5%)
  other arithmetic  10.5 us (4%)
  starting transfers between devices  9.38 us (3%)
    pmax x1, blocking collectives, shards(): global_max = lax.pmax(maxima, 'seq')  66.3 us
    psum x1, blocking collectives, shards(): lax.psum((totals * factor).astype(jnp.bfloat16), 'seq').astype(jnp.float32)  62.8 us
    psum x1, waiting for transfers between devices, shards(): lax.psum(scale_rows(partial_value, factor).astype(jnp.bfloat16), 'seq')  38.6 us
    all_gather x1, blocking collectives, shards(): queries_all = lax.all_gather(queries, 'seq', axis=0, tiled=True)  26.5 us
    reduce_scatter x1, waiting for transfers between devices, shards(): lax.psum_scatter(jnp.dot(attended, w_out, preferred_element_type=jnp.floa...  20.4 us
    dot_general x1, matrix products, shards(): jnp.dot(vision, w_value, preferred_element_type=jnp.float32)  10.6 us
    dot_general x1, matrix products, shards(): jnp.dot(vision, w_key, preferred_element_type=jnp.float32)  10.5 us
    reduce_sum x1, other arithmetic, attend(): totals = jnp.sum(powers, axis=-1)  8.48 us
  transfers between devices with their start and end apart: 4, of which 2 were waited for; matrix products, arithmetic and copies ran while one was open for 4% of the time, Pallas kernels for 0%

commit v1 on v0

--- a/solution.py
+++ b/solution.py
@@ -57,7 +57,9 @@
     global_max = lax.pmax(maxima, "seq")
     factor = jnp.exp(maxima - global_max)
     denom, numer = (
-        lax.psum((totals * factor).astype(jnp.bfloat16), "seq").astype(jnp.float32),
+        jnp.sum(lax.all_gather((totals * factor).astype(jnp.bfloat16), "seq"), axis=0).astype(
+            jnp.float32
+        ),
         lax.psum(scale_rows(partial_value, factor).astype(jnp.bfloat16), "seq").astype(jnp.float32),
     )
     attended = divide_rows(numer, denom).astype(jnp.bfloat16)

time: 287 us -> 288 us (level)
  blocking collectives: 156 us -> 114 us
  waiting for transfers between devices: 59 us -> 101 us
    psum x1 -> x0, blocking collectives: 62.8 us -> none  [shards(): lax.psum((totals * factor).astype(jnp.bfloat16), 'seq').astype(jnp.float32)]
    psum x1, waiting for transfers between devices: 38.6 us -> 80.7 us  [shards(): lax.psum(scale_rows(partial_value, factor).astype(jnp.bfloat16), 'seq')]
    all_gather x0 -> x1, blocking collectives: none -> 21.1 us  [shards(): lax.all_gather((totals * factor).astype(jnp.bfloat16), 'seq')]
where the time goes in v1:
time: 288 us; the launch traced here: 287 us
  blocking collectives  114 us (40%)
  waiting for transfers between devices  101 us (35%)
  matrix products  37.6 us (13%)
  between operations  13.5 us (5%)
  other arithmetic  10.6 us (4%)
  starting transfers between devices  9.38 us (3%)
    psum x1, waiting for transfers between devices, shards(): lax.psum(scale_rows(partial_value, factor).astype(jnp.bfloat16), 'seq')  80.7 us
    pmax x1, blocking collectives, shards(): global_max = lax.pmax(maxima, 'seq')  66.3 us
    all_gather x1, blocking collectives, shards(): queries_all = lax.all_gather(queries, 'seq', axis=0, tiled=True)  26.5 us
    all_gather x1, blocking collectives, shards(): lax.all_gather((totals * factor).astype(jnp.bfloat16), 'seq')  21.1 us
    reduce_scatter x1, waiting for transfers between devices, shards(): lax.psum_scatter(jnp.dot(attended, w_out, preferred_element_type=jnp.floa...  20.4 us
    dot_general x1, matrix products, shards(): jnp.dot(vision, w_value, preferred_element_type=jnp.float32)  10.6 us
    dot_general x1, matrix products, shards(): jnp.dot(vision, w_key, preferred_element_type=jnp.float32)  10.5 us
    reduce_sum x1, other arithmetic, attend(): totals = jnp.sum(powers, axis=-1)  8.48 us
  transfers between devices with their start and end apart: 4, of which 2 were waited for; matrix products, arithmetic and copies ran while one was open for 4% of the time, Pallas kernels for 0%

profile of v1, /device:TPU:0, one launch (start us, length us, event | category | flops | bytes accessed | tf_op | source)
XLA Modules:
  0.0 287.3 jit_solution(17784836179455780720)
XLA Ops:
  6.5 0.0 copy-start
  6.5 10.6 %convolution_convert_fusion.1 = bf16[512,512]{0,1:T(8,128)(2,1)} fusion(bf16[512,7680]{1,0:T(8,128)(2,1)} %param.5, bf16[7680,512]{1,0:T(8,128)(2,1)} %param.7), kind=kOutput, calls=%fused_computation.8 | convolution fusion | flops 4026793984 | bytes 16252928 | tf_op jit(solution)/shard_map/dot_general | solution.py:50
  17.1 0.0 copy-start.1
  17.1 4.5 %all-to-all-start = ((bf16[512,4,128]{0,2,1:T(8,128)(2,1)}), bf16[512,4,128]{0,2,1:T(8,128)(2,1)S(1)}, u32[]{:S(2)}, u32[]{:S(2)}) async-start(bf16[512,4,128]{0,2,1:T(8,128)(2,1)} %bitcast), calls=%async_computation | async-start | bytes 1048576 | tf_op jit(solution)/shard_map/all_to_all | solution.py:53
  21.7 10.5 %convolution_convert_fusion = bf16[512,512]{0,1:T(8,128)(2,1)} fusion(bf16[512,7680]{1,0:T(8,128)(2,1)} %param.5, bf16[7680,512]{1,0:T(8,128)(2,1)} %param.6), kind=kOutput, calls=%fused_computation.7 | convolution fusion | flops 4026793984 | bytes 16252928 | tf_op jit(solution)/shard_map/dot_general | solution.py:49
  32.2 0.0 all-to-all-done
  32.2 4.8 %all-to-all-start.1 = ((bf16[512,4,128]{0,2,1:T(8,128)(2,1)}), bf16[512,4,128]{0,2,1:T(8,128)(2,1)S(1)}, u32[]{:S(2)}, u32[]{:S(2)}) async-start(bf16[512,4,128]{0,2,1:T(8,128)(2,1)} %bitcast.2), calls=%async_computation.1 | async-start | bytes 1048576 | tf_op jit(solution)/shard_map/all_to_all | solution.py:52
  37.0 0.0 all-reduce.2.cloned.1.call-start
  37.0 0.0 copy-done.1
  37.0 26.5 %all_gather.9 = bf16[256,1024]{1,0:T(8,128)(2,1)S(1)} all-gather(bf16[8,1024]{1,0:T(8,128)(2,1)S(1)} %copy-done.1), channel_id=1, replica_groups=mesh['seq'=32,'head'=4] {'seq'}, dimensions={0}, use_global_device_ids=true | all-gather | bytes 540672 | tf_op jit(solution)/shard_map/all_gather | solution.py:55
  63.5 0.2 copy.16
  63.7 0.4 copy.14
  64.1 0.4 reshape.60
  64.5 0.0 all-to-all-done.1
  64.5 0.3 copy.15
  64.8 8.0 %bitcast_reduce_fusion = (f32[8,256]{1,0:T(8,128)S(1)}, f32[2048,256,8]{1,0,2:T(8,128)}) fusion(bf16[2048,128,1]{1,0,2:T(8,128)(2,1)S(1)} %bitcast.67, bf16[256,8,128]{0,2,1:T(8,128)(2,1)S(1)} %bitcast.66), kind=kOutput, calls=%fused_computation.1 | convolution fusion | flops 1082128384 | bytes 17833984 | tf_op jit(solution)/shard_map/tkgd,nkd->kgtn/dot_general | solution.py:30
  72.8 8.5 %fusion.1 = f32[8,256]{1,0:T(8,128)S(1)} fusion(f32[2048,256,8]{1,0,2:T(8,128)} %get-tuple-element.8, f32[8,256]{1,0:T(8,128)S(1)} %get-tuple-element.7), kind=kLoop, calls=%fused_computation.3 | loop fusion | flops 12580864 | bytes 16793600 | tf_op jit(solution)/shard_map/reduce_sum | solution.py:35
  81.3 7.4 %fusion.4 = f32[128,8,256]{2,0,1:T(8,128)S(1)} fusion(bf16[2048,128,1]{0,1,2:T(8,128)(2,1)S(1)} %reshape.60, f32[2048,256,8]{1,0,2:T(8,128)} %get-tuple-element.8, f32[8,256]{1,0:T(8,128)S(1)} %get-tuple-element.7), kind=kOutput, calls=%fused_computation.6 | convolution fusion | flops 1086324736 | bytes 18358272 | tf_op jit(solution)/shard_map/kgtn,nkd->tkgd/dot_general | solution.py:36
  88.7 66.3 %pmax.7 = f32[256,8]{0,1:T(8,128)S(1)} all-reduce(f32[256,8]{0,1:T(8,128)S(1)} %bitcast.71), channel_id=1, replica_groups=mesh['seq'=32,'head'=4] {'seq'}, use_global_device_ids=true, to_apply=%region_1.0 | all-reduce | flops 2048 | bytes 16384 | tf_op jit(solution)/shard_map/pmax | solution.py:57
  155.1 0.9 fusion.6
  156.0 0.0 all-reduce.2.cloned.1.call-update
  156.0 0.0 reduce-scatter.2.cloned.1.call-start
  156.0 21.1 %all-gather = bf16[8192,8]{0,1:T(8,128)(2,1)S(1)} all-gather(bf16[256,8]{0,1:T(8,128)(2,1)S(1)} %get-tuple-element.5), channel_id=2, replica_groups=mesh['seq'=32,'head'=4] {'seq'}, dimensions={0}, use_global_device_ids=true | all-gather | bytes 135168 | tf_op jit(solution)/shard_map/all_gather | solution.py:60
  177.2 80.7 %all-reduce.2.cloned.1.call-done = bf16[256,1024]{0,1:T(8,128)(2,1)} async-done(((bf16[256,1024]{0,1:T(8,128)(2,1)}), bf16[256,1024]{0,1:T(8,128)(2,1)}) %all-reduce.2.cloned.1.call-update) | async-done | bytes 524304 | tf_op jit(solution)/shard_map/psum | solution.py:63
  257.9 1.1 fusion.7
  259.0 0.0 copy-done
  259.0 1.0 convolution_convert_fusion.2
  260.0 0.0 reduce-scatter.2.cloned.1.call-update
  260.0 20.4 %reduce-scatter.2.cloned.1.call-done = bf16[64,256]{1,0:T(8,128)(2,1)} async-done(((bf16[256,256]{1,0:T(8,128)(2,1)}), bf16[64,256]{1,0:T(8,128)(2,1)}) %reduce-scatter.2.cloned.1.call-update) | async-done | bytes 32784 | tf_op jit(solution)/shard_map/reduce_scatter | solution.py:66
  (3 shorter events, 0.1 us)
Async XLA Ops:
  6.5 252.5 %copy-start = (bf16[1024,256]{1,0:T(8,128)(2,1)S(1)}, bf16[1024,256]{1,0:T(8,128)(2,1)}, u32[]{:S(2)}) copy-start(bf16[1024,256]{1,0:T(8,128)(2,1)} %param.9) | copy-start | bytes 1572868
  17.1 19.9 %copy-start.1 = (bf16[8,1024]{1,0:T(8,128)(2,1)S(1)}, bf16[8,1024]{1,0:T(8,128)(2,1)}, u32[]{:S(2)}) copy-start(bf16[8,1024]{1,0:T(8,128)(2,1)} %param.8) | copy-start | bytes 49156
  17.1 15.1 %all-to-all-start = ((bf16[512,4,128]{0,2,1:T(8,128)(2,1)}), bf16[512,4,128]{0,2,1:T(8,128)(2,1)S(1)}, u32[]{:S(2)}, u32[]{:S(2)}) async-start(bf16[512,4,128]{0,2,1:T(8,128)(2,1)} %bitcast), calls=%async_computation | async-start | bytes 1048576 | tf_op jit(solution)/shard_map/all_to_all | solution.py:53
  32.2 32.3 %all-to-all-start.1 = ((bf16[512,4,128]{0,2,1:T(8,128)(2,1)}), bf16[512,4,128]{0,2,1:T(8,128)(2,1)S(1)}, u32[]{:S(2)}, u32[]{:S(2)}) async-start(bf16[512,4,128]{0,2,1:T(8,128)(2,1)} %bitcast.2), calls=%async_computation.1 | async-start | bytes 1048576 | tf_op jit(solution)/shard_map/all_to_all | solution.py:52
  37.0 220.9 %all-reduce.2.cloned.1.call-start = ((), (), s32[]{:S(2)}) async-start(), calls=%async_computation.3 | async-start | bytes 1048576 | tf_op jit(solution)/shard_map/psum | solution.py:63
  156.0 124.4 %reduce-scatter.2.cloned.1.call-start = ((), (), s32[]{:S(2)}) async-start(), calls=%async_computation.4 | async-start | bytes 163840 | tf_op jit(solution)/shard_map/reduce_scatter | solution.py:66
Sparse Core Ops, SparseCore 0:
  156.1 101.7 all-reduce.1
  260.2 20.1 reduce-scatter.1
